TPU v7x, 32 devices: a whole 2x2x4 slice. The times are simulated.
32 devices in a mesh: hist: 4 (over y, x), tcol: 8 (over z, core).
Axes of the slice: x: 2, y: 2, z: 4, core: 2. Of those that a mesh axis runs over, the one named last changes fastest.
Arguments:
- history: float32 [8192, 4096], P('hist', 'tcol'), may hold values from -5 to 5
- memory_weight_first: float32 [512, 8192], P(None, 'hist'), may hold values from -0.09375 to 0.09375
- memory_weight_second: float32 [512, 8192], P(None, 'hist'), may hold values from -0.09375 to 0.09375
- link: float32 [512, 512], replicated, may hold values from -0.25 to 0.25
- propagator: float32 [4096, 4096], P(None, 'tcol'), may hold values from -0.09375 to 0.09375
- inverse_one: float32 [512, 512], replicated, as said below
- inverse_two: float32 [512, 512], replicated, as said below
- explicit_first: float32 [512, 4096], P(None, 'tcol'), may hold values from -5 to 5
- explicit_second: float32 [512, 4096], P(None, 'tcol'), may hold values from -5 to 5
Outputs:
- first_slab_rows: float32 [512, 4096], P('hist', 'tcol')
- slab_two: float32 [512, 4096], P('hist', 'tcol')
Inputs may be any that keep to these rules, and one draw needn't show every extreme that they name: `inverse_one`: the identity plus independent entries of deviation 0.5 / sqrt(512). `inverse_two`: the identity plus independent entries of deviation 0.5 / sqrt(512).
All inputs are finite; a program needn't handle non-finite values.
Results may differ from a plain program's by a relative error of at most 0.0003.
Values sent between devices are 32-bit elements; how exact they have to be, the bound alone decides.
A program may use at most 128 MiB of HBM per device.

v0:
```python
import jax
import jax.numpy as jnp
from jax import lax
from jax.sharding import PartitionSpec as P

strength = 0.2
step_size = 0.5
highest = lax.Precision.HIGHEST


def cubic_power(value):
    return strength * value * value * value


def matrix_product(left, right):
    return jnp.dot(left, right, preferred_element_type=jnp.float32, precision=highest)


def shards(
    history,
    memory_weight_first,
    memory_weight_second,
    link,
    propagator,
    inverse_one,
    inverse_two,
    explicit_first,
    explicit_second,
):
    self_energy_history = cubic_power(history)
    parts = lax.axis_size("hist")
    rows = memory_weight_first.shape[0] // parts
    offset = lax.axis_index("hist") * rows

    def memory(sigma_rows):
        return matrix_product(lax.all_gather(sigma_rows, "tcol", axis=1, tiled=True), propagator)

    own_source_one = lax.dynamic_slice_in_dim(explicit_first, offset, rows, 0)
    own_source_two = lax.dynamic_slice_in_dim(explicit_second, offset, rows, 0)
    predictor_first = own_source_one + lax.psum_scatter(
        matrix_product(memory_weight_first, self_energy_history),
        "hist",
        scatter_dimension=0,
        tiled=True,
    )
    right_one = predictor_first + step_size * memory(cubic_power(predictor_first))
    block = lax.dynamic_slice(inverse_one, (0, offset), (lax.axis_size("hist") * rows, rows))
    first_slab_rows = lax.psum_scatter(
        matrix_product(block, right_one), "hist", scatter_dimension=0, tiled=True
    )
    sigma_one = cubic_power(first_slab_rows)
    near = matrix_product(memory_weight_second, self_energy_history)
    block = lax.dynamic_slice(link, (0, offset), (lax.axis_size("hist") * rows, rows))
    predictor_second = own_source_two + lax.psum_scatter(
        near + matrix_product(block, sigma_one), "hist", scatter_dimension=0, tiled=True
    )
    right_two = predictor_second + step_size * memory(cubic_power(predictor_second))
    block = lax.dynamic_slice(inverse_two, (0, offset), (lax.axis_size("hist") * rows, rows))
    slab_two = lax.psum_scatter(
        matrix_product(block, right_two), "hist", scatter_dimension=0, tiled=True
    )
    return (first_slab_rows, slab_two)


def solution(mesh):
    return jax.shard_map(
        shards,
        mesh=mesh,
        in_specs=(
            P("hist", "tcol"),
            P(None, "hist"),
            P(None, "hist"),
            P(),
            P(None, "tcol"),
            P(),
            P(),
            P(None, "tcol"),
            P(None, "tcol"),
        ),
        out_specs=(P("hist", "tcol"), P("hist", "tcol")),
        check_vma=False,
    )
```

profile of v0, /device:TPU:1, one launch (start us, length us, event | category | flops | bytes accessed | tf_op | source)
XLA Modules:
  0.0 246.3 jit_solution(17302326417263502843)
XLA Ops:
  7.2 0.0 copy-start
  7.2 0.0 reduce-scatter.5.cloned.1.call-start
  7.2 16.8 %fusion.4 = f32[512,512]{0,1:T(8,128)} fusion(f32[512,2048]{1,0:T(8,128)} %param.10, f32[2048,512]{1,0:T(8,128)} %param.9), kind=kOutput, calls=%fused_computation.5 | convolution fusion | flops 6445596672 | bytes 9437184 | tf_op jit(solution)/shard_map/dot_general | solution.py:16
  24.0 0.0 reduce-scatter.5.cloned.1.call-update
  24.0 0.0 all-gather.3.cloned.1.call-start
  24.1 1.0 constant_dynamic-slice_fusion.1
  25.1 0.1 copy.18
  25.2 28.8 %reduce-scatter.5.cloned.1.call-done = f32[128,512]{0,1:T(8,128)} async-done(((f32[512,512]{0,1:T(8,128)}), f32[128,512]{0,1:T(8,128)}) %reduce-scatter.5.cloned.1.call-update) | async-done | bytes 262160 | tf_op jit(solution)/shard_map/reduce_scatter | solution.py:40
  54.0 1.7 multiply_multiply_fusion.9
  55.7 0.0 all-gather.3.cloned.1.call-update
  55.7 0.2 reduce-scatter.7.cloned.1.call-start
  56.0 30.0 %all-gather.3.cloned.1.call-done = f32[128,4096]{0,1:T(8,128)} async-done(((f32[128,512]{0,1:T(8,128)}), f32[128,4096]{0,1:T(8,128)}) %all-gather.3.cloned.1.call-update) | async-done | bytes 2097168 | tf_op jit(solution)/shard_map/all_gather | solution.py:36
  85.9 15.9 %fusion.7 = f32[128,512]{0,1:T(8,128)S(1)} fusion(f32[128,512]{0,1:T(8,128)S(1)} %get-tuple-element.7, f32[128,4096]{0,1:T(8,128)} %all-gather.3.cloned.1.call-done, f32[4096,512]{1,0:T(8,128)} %param.13), kind=kOutput, calls=%fused_computation.11 | convolution fusion | flops 3221356544 | bytes 11010048 | tf_op jit(solution)/shard_map/dot_general | solution.py:16
  101.8 0.0 copy-done
  101.8 2.0 fusion.11
  103.8 0.0 reduce-scatter.7.cloned.1.call-update
  103.8 0.3 reduce-scatter.9.cloned.1.call-start
  104.1 15.8 %fusion.5 = f32[512,512]{0,1:T(8,128)S(1)} fusion(f32[512,2048]{1,0:T(8,128)} %param.11, f32[2048,512]{1,0:T(8,128)} %param.9), kind=kOutput, calls=%fused_computation.6 | convolution fusion | flops 6445596672 | bytes 9437184 | tf_op jit(solution)/shard_map/dot_general | solution.py:16
  119.9 10.9 %reduce-scatter.7.cloned.1.call-done = f32[128,512]{0,1:T(8,128)} async-done(((f32[512,512]{0,1:T(8,128)}), f32[128,512]{0,1:T(8,128)}) %reduce-scatter.7.cloned.1.call-update) | async-done | bytes 262160 | tf_op jit(solution)/shard_map/reduce_scatter | solution.py:48
  130.8 3.0 %convolution_add_fusion = f32[512,512]{0,1:T(8,128)} fusion(f32[512,512]{0,1:T(8,128)S(1)} %fusion.5, f32[128,512]{0,1:T(8,128)} %reduce-scatter.7.cloned.1.call-done, f32[512,512]{1,0:T(8,128)} %param.12, s32[]{:T(128)S(6)} %select_n.2), kind=kOutput, calls=%fused_computation.7 | convolution fusion | flops 403111936 | bytes 2621444 | tf_op jit(solution)/shard_map/dot_general | solution.py:16
  133.8 0.0 reduce-scatter.9.cloned.1.call-update
  133.8 0.0 all-gather.5.cloned.1.call-start
  133.9 1.0 constant_dynamic-slice_fusion
  134.8 0.1 copy.19
  135.0 26.9 %reduce-scatter.9.cloned.1.call-done = f32[128,512]{0,1:T(8,128)} async-done(((f32[512,512]{0,1:T(8,128)}), f32[128,512]{0,1:T(8,128)}) %reduce-scatter.9.cloned.1.call-update) | async-done | bytes 262160 | tf_op jit(solution)/shard_map/reduce_scatter | solution.py:54
  161.9 1.7 multiply_multiply_fusion.7
  163.6 0.0 all-gather.5.cloned.1.call-update
  163.6 0.3 reduce-scatter.11.cloned.1.call-start
  163.9 29.7 %all-gather.5.cloned.1.call-done = f32[128,4096]{0,1:T(8,128)} async-done(((f32[128,512]{0,1:T(8,128)}), f32[128,4096]{0,1:T(8,128)}) %all-gather.5.cloned.1.call-update) | async-done | bytes 2097168 | tf_op jit(solution)/shard_map/all_gather | solution.py:36
  193.7 0.0 copy-start.1
  193.7 15.9 %fusion.6 = f32[128,512]{0,1:T(8,128)S(1)} fusion(f32[128,512]{0,1:T(8,128)S(1)} %get-tuple-element.5, f32[128,4096]{0,1:T(8,128)} %all-gather.5.cloned.1.call-done, f32[4096,512]{1,0:T(8,128)} %param.13), kind=kOutput, calls=%fused_computation.9 | convolution fusion | flops 3221356544 | bytes 11010048 | tf_op jit(solution)/shard_map/dot_general | solution.py:16
  209.6 2.9 %fusion.9 = f32[512,512]{1,0:T(8,128)} fusion(f32[128,512]{0,1:T(8,128)S(1)} %fusion.6, f32[512,512]{1,0:T(8,128)} %param.15, s32[]{:T(128)S(6)} %select_n.2), kind=kOutput, calls=%fused_computation.16 | convolution fusion | flops 402653184 | bytes 1572868 | tf_op jit(solution)/shard_map/dot_general | solution.py:16
  212.5 0.0 reduce-scatter.11.cloned.1.call-update
  212.5 0.0 copy-done.1
  212.5 0.8 copy.15
  213.4 26.1 %reduce-scatter.11.cloned.1.call-done = f32[128,512]{1,0:T(8,128)} async-done(((f32[512,512]{1,0:T(8,128)}), f32[128,512]{1,0:T(8,128)}) %reduce-scatter.11.cloned.1.call-update) | async-done | bytes 262160 | tf_op jit(solution)/shard_map/reduce_scatter | solution.py:59
Async XLA Ops:
  7.2 94.7 %copy-start = (f32[512,512]{1,0:T(8,128)S(1)}, f32[512,512]{1,0:T(8,128)}, u32[]{:S(2)}) copy-start(f32[512,512]{1,0:T(8,128)} %param.14) | copy-start | bytes 3145732
  7.2 46.9 %reduce-scatter.5.cloned.1.call-start = ((), (), s32[]{:S(2)}) async-start(), calls=%async_computation.4 | async-start | bytes 1310720 | tf_op jit(solution)/shard_map/reduce_scatter | solution.py:40
  24.0 61.9 %all-gather.3.cloned.1.call-start = ((), (), s32[]{:S(2)}) async-start(), calls=%async_computation.5 | async-start | bytes 2359296 | tf_op jit(solution)/shard_map/all_gather | solution.py:36
  55.7 75.0 %reduce-scatter.7.cloned.1.call-start = ((), (), s32[]{:S(2)}) async-start(), calls=%async_computation.6 | async-start | bytes 1310720 | tf_op jit(solution)/shard_map/reduce_scatter | solution.py:48
  103.8 58.0 %reduce-scatter.9.cloned.1.call-start = ((), (), s32[]{:S(2)}) async-start(), calls=%async_computation.7 | async-start | bytes 1310720 | tf_op jit(solution)/shard_map/reduce_scatter | solution.py:54
  133.8 59.8 %all-gather.5.cloned.1.call-start = ((), (), s32[]{:S(2)}) async-start(), calls=%async_computation.8 | async-start | bytes 2359296 | tf_op jit(solution)/shard_map/all_gather | solution.py:36
  163.6 75.9 %reduce-scatter.11.cloned.1.call-start = ((), (), s32[]{:S(2)}) async-start(), calls=%async_computation.9 | async-start | bytes 1310720 | tf_op jit(solution)/shard_map/reduce_scatter | solution.py:59
  193.7 18.9 %copy-start.1 = (f32[128,512]{0,1:T(8,128)S(1)}, f32[128,512]{0,1:T(8,128)}, u32[]{:S(2)}) copy-start(f32[128,512]{0,1:T(8,128)} %reduce-scatter.7.cloned.1.call-done) | copy-start | bytes 786436
Sparse Core Ops, SparseCore 0:
  24.2 29.8 reduce-scatter.4
  56.2 29.6 all-gather.2
  104.0 26.7 reduce-scatter.6
  133.9 27.9 reduce-scatter.8
  163.9 29.6 all-gather.4
  212.6 26.7 reduce-scatter.10
where the time goes:
time: 247 us; the launch traced here: 246 us
  waiting for transfers between devices  153 us (62%)
  matrix products  72.3 us (29%)
  between operations  14.2 us (6%)
  other arithmetic  3.38 us (1%)
  local copies, waits for them, and re-layouts  3.04 us (1%)
    dot_general x7, matrix products, matrix_product(): jnp.dot(left, right, preferred_element_type=jnp.float32, precision=highest)  72.3 us
    all_gather x2, waiting for transfers between devices, memory(): lax.all_gather(sigma_rows, 'tcol', axis=1, tiled=True)  59.7 us
    reduce_scatter x1, waiting for transfers between devices, shards(): lax.psum_scatter(matrix_product(memory_weight_first, self_energy_history)...  28.8 us
    reduce_scatter x1, waiting for transfers between devices, shards(): lax.psum_scatter(near + matrix_product(block, sigma_one), 'hist', scatter...  26.9 us
    reduce_scatter x1, waiting for transfers between devices, shards(): lax.psum_scatter(matrix_product(block, right_two), 'hist', scatter_dimens...  26.1 us
    reduce_scatter x1, waiting for transfers between devices, shards(): lax.psum_scatter(matrix_product(block, right_one), 'hist', scatter_dimens...  10.9 us
  transfers between devices with their start and end apart: 6, of which 6 were waited for; matrix products, arithmetic and copies ran while one was open for 8% of the time, Pallas kernels for 0%

commit v1 on v0

v1 whole, which is shorter than its diff:
```python
import functools

import jax
import jax.numpy as jnp
from jax import lax
from jax.experimental import pallas as pl
from jax.experimental.pallas import tpu as pltpu
from jax.sharding import PartitionSpec as P

strength = 0.2
step_size = 0.5
MESH = pl.DeviceIdType.MESH
f32 = jnp.float32
bf16 = jnp.bfloat16


def cubic_power(value):
    return strength * value * value * value


def halves(value):
    high = value.astype(bf16)
    return high, (value - high.astype(f32)).astype(bf16)


def mm(left, right):
    return jnp.dot(left, right, preferred_element_type=f32)


def product(left, right_high, right_low):
    m = left.shape[0]
    high, low = halves(left)
    both = mm(jnp.concatenate([high, low], axis=0), right_high)
    return both[:m] + both[m:] + mm(high, right_low)


def kernel(
    H, T, C,
    hist_ref, w1_ref, w2_ref, link_ref, prop_ref, inv1_ref, inv2_ref, e1_ref, e2_ref,
    o1_ref, o2_ref,
    hbuf, wbuf, wh, wl, sh, sl, ph, plo, mat, ih, il, kh, kl, inv2, e1, e2,
    part, rs, pred, acc1, g1, g2, rf, nf, xh, xl, s1, p2h, p2l, qh, ql, base,
    hsem, wsem, psem, msem, rs_send, rs_recv, rf_send, rf_recv, nf_send, nf_recv,
    sp, sr, sleft, rz, rp,
):
    K, N = hist_ref.shape
    S = w1_ref.shape[0]
    R = S // H
    Rc = R // C
    Nc = N // C
    nK = K // N
    Z = T // 2
    h = lax.axis_index("hist")
    t = lax.axis_index("tcol")
    p = t // 2
    core = t % 2
    other = 1 - core
    tile = 32

    def split(source, high, low, rows, function=lambda v: v):
        @pl.loop(0, rows // tile)
        def _(i):
            at = pl.ds(pl.multiple_of(i * tile, tile), tile)
            a, b = halves(function(source[at, :]))
            high[at, :] = a
            low[at, :] = b

    def hist_copy(kb):
        return pltpu.make_async_copy(hist_ref.at[pl.ds(kb * N, N), :], hbuf.at[kb], hsem.at[kb])

    def w_copy(w, c, j):
        ref = (w1_ref, w2_ref)[w]
        return pltpu.make_async_copy(
            ref.at[pl.ds(j * R + c * Rc, Rc), :], wbuf.at[w, c, j], wsem.at[w, c, j]
        )

    def p_copy(b):
        return pltpu.make_async_copy(
            prop_ref.at[pl.ds(b * N, N), :], hbuf.at[b % nK], psem.at[b]
        )

    own_rows = pl.ds(pl.multiple_of(h * R, R), R)
    small = (
        pltpu.make_async_copy(e1_ref.at[own_rows, :], e1, msem.at[0]),
        pltpu.make_async_copy(inv1_ref, mat.at[0], msem.at[1]),
        pltpu.make_async_copy(link_ref, mat.at[1], msem.at[2]),
        pltpu.make_async_copy(inv2_ref.at[own_rows, :], inv2, msem.at[3]),
        pltpu.make_async_copy(e2_ref, e2, msem.at[4]),
    )

    for kb in range(nK):
        hist_copy(kb).start()
    for c in range(C):
        for j in range(H):
            w_copy(0, c, j).start()
    small[0].start()

    barrier = pltpu.get_barrier_semaphore()

    def greet(device):
        pl.semaphore_signal(barrier, inc=1, device_id=device, device_id_type=MESH)

    for d in range(1, H):
        greet({"hist": lax.rem(h + d, H)})
    greet({"tcol": p * 2 + other})

    greet({"tcol": lax.rem(p + 1, Z) * 2 + core})
    greet({"tcol": lax.rem(p + Z - 1, Z) * 2 + core})

    for kb in range(nK):
        hist_copy(kb).wait()
        split(hbuf.at[kb], sh.at[kb], sl.at[kb], N, cubic_power)

    for c in range(C):
        for j in range(H):
            w_copy(1, c, j).start()
    for copy in small[1:]:
        copy.start()
    for b in range(nK):
        p_copy(b).start()

    def history_sum(w, c):
        for j in range(H):
            w_copy(w, c, j).wait()
            split(wbuf.at[w, c, j], wh.at[j], wl.at[j], Rc)

        for kb in range(nK):
            cols = pl.ds(kb * N, N)
            a = wh[:, :, cols].reshape(H * Rc, N)
            b = wl[:, :, cols].reshape(H * Rc, N)
            value = mm(a, sh[kb]) + mm(b, sh[kb]) + mm(a, sl[kb])
            value = value.reshape(H, Rc, N)
            if kb == 0:
                part[w, c] = value
            else:
                part[w, c] += value

    def rs_copy(w, c, d):
        dst = lax.rem(h + d, H)
        return pltpu.make_async_remote_copy(
            src_ref=part.at[w, c, dst], dst_ref=rs.at[w, c, d - 1],
            send_sem=rs_send.at[w, c, d - 1], recv_sem=rs_recv.at[w, c, d - 1],
            device_id={"hist": dst}, device_id_type=MESH,
        )

    def gathered(w, c):
        total = part[w, c, h]
        for d in range(1, H):
            rs_copy(w, c, d).wait_recv()
            total += rs[w, c, d - 1]
        return total

    def z_copy(g, st, c, q, where):
        block = g.at[c, 2 * q + core]
        send, recv, target = {
            "partner": (sp, rp, p * 2 + other),
            "right": (sr, rz, t + 2),
            "left": (sleft, rz, t - 2),
        }[where]
        return pltpu.make_async_remote_copy(
            src_ref=block, dst_ref=block,
            send_sem=send.at[st, c, q], recv_sem=recv.at[st, c, q],
            device_id={"tcol": target}, device_id_type=MESH,
        )

    def z_partner_wait(g, st, c, q):
        block = g.at[c, 2 * q + other]
        pltpu.make_async_remote_copy(
            src_ref=block, dst_ref=block,
            send_sem=sp.at[st, c, q], recv_sem=rp.at[st, c, q],
            device_id={"tcol": p * 2 + other}, device_id_type=MESH,
        ).wait_recv()

    def z_own(g, st, c):
        @pl.when(p + 1 < Z)
        def _():
            z_copy(g, st, c, p, "right").start()

        @pl.when(p > 0)
        def _():
            z_copy(g, st, c, p, "left").start()

        z_copy(g, st, c, p, "partner").start()

    def z_step(g, st, c, s, use):
        @pl.when(p >= s)
        def _():
            q = p - s
            z_copy(g, st, c, q, "right").wait_recv()

            @pl.when(p + 1 < Z)
            def _():
                z_copy(g, st, c, q, "right").start()

            z_copy(g, st, c, q, "partner").start()

        @pl.when(p + s < Z)
        def _():
            q = p + s
            z_copy(g, st, c, q, "left").wait_recv()

            @pl.when(p > 0)
            def _():
                z_copy(g, st, c, q, "left").start()

            z_copy(g, st, c, q, "partner").start()

        @pl.when(p >= s)
        def _():
            use(c, 2 * (p - s) + core)

        @pl.when(p + s < Z)
        def _():
            use(c, 2 * (p + s) + core)

        @pl.when(p >= s)
        def _():
            z_partner_wait(g, st, c, p - s)
            use(c, 2 * (p - s) + other)

        @pl.when(p + s < Z)
        def _():
            z_partner_wait(g, st, c, p + s)
            use(c, 2 * (p + s) + other)

    def z_finish(g, st, c):
        z_copy(g, st, c, p, "partner").wait_send()

        @pl.when(p + 1 < Z)
        def _():
            z_copy(g, st, c, p, "right").wait_send()

        @pl.when(p > 0)
        def _():
            z_copy(g, st, c, p, "left").wait_send()

        for s in range(1, Z):
            @pl.when(p >= s)
            def _():
                z_copy(g, st, c, p - s, "partner").wait_send()

                @pl.when(p + 1 < Z)
                def _():
                    z_copy(g, st, c, p - s, "right").wait_send()

            @pl.when(p + s < Z)
            def _():
                z_copy(g, st, c, p + s, "partner").wait_send()

                @pl.when(p > 0)
                def _():
                    z_copy(g, st, c, p + s, "left").wait_send()

    def use_one(c, b):
        acc1[c] += product(g1[c, b], ph[b], plo[b])

    def use_two(c, b):
        rows = pl.ds(c * Nc, Nc)
        base[...] += product(g2[c, b], ph[b, rows, :], plo[b, rows, :])

    history_sum(0, 0)
    pl.semaphore_wait(barrier, H + 2)

    for d in range(1, H):
        rs_copy(0, 0, d).start()
    for c in range(1, C):
        history_sum(0, c)
        for d in range(1, H):
            rs_copy(0, c, d).start()

    small[0].wait()

    def begin_one(c):
        value = gathered(0, c) + e1[pl.ds(c * Rc, Rc), :]
        pred[c] = value
        g1[c, t] = cubic_power(value)
        z_own(g1, 0, c)

    for c in range(C):
        history_sum(1, c)
        for d in range(1, H):
            rs_copy(1, c, d).start()
        if c == 0:
            begin_one(0)

    for b in range(T):
        p_copy(b).wait()
        split(hbuf.at[b % nK], ph.at[b], plo.at[b], N)
        if b + nK < T:
            p_copy(b + nK).start()

    def local_one(c):
        acc1[c] = product(g1[c, t], ph[t], plo[t])
        z_partner_wait(g1, 0, c, p)
        use_one(c, 2 * p + other)

    local_one(0)
    for c in range(1, C):
        if c == 1:
            z_step(g1, 0, 0, 1, use_one)
        begin_one(c)
        local_one(c)
        z_step(g1, 0, c, 1, use_one)

    for copy in small[1:]:
        copy.wait()
    split(mat.at[0], ih, il, S)
    split(mat.at[1], kh, kl, S)

    def nf_copy(d):
        dst = lax.rem(h + d, H)
        return pltpu.make_async_remote_copy(
            src_ref=nf.at[h], dst_ref=nf.at[h],
            send_sem=nf_send.at[d - 1], recv_sem=nf_recv.at[d - 1],
            device_id={"hist": dst}, device_id_type=MESH,
        )

    def nf_wait(d):
        src = lax.rem(h + H - d, H)
        pltpu.make_async_remote_copy(
            src_ref=nf.at[src], dst_ref=nf.at[src],
            send_sem=nf_send.at[d - 1], recv_sem=nf_recv.at[d - 1],
            device_id={"hist": src}, device_id_type=MESH,
        ).wait_recv()

    for s in range(2, Z):
        for c in range(C):
            z_step(g1, 0, c, s, use_one)
        if s == max(2, Z // 2):
            for c in range(C):
                nf[h, pl.ds(c * Rc, Rc), :] = gathered(1, c)
            for d in range(1, H):
                nf_copy(d).start()

    def rf_copy(c, d):
        dst = lax.rem(h + d, H)
        return pltpu.make_async_remote_copy(
            src_ref=rf.at[c, h], dst_ref=rf.at[c, h],
            send_sem=rf_send.at[c, d - 1], recv_sem=rf_recv.at[c, d - 1],
            device_id={"hist": dst}, device_id_type=MESH,
        )

    def rf_wait(c, d):
        src = lax.rem(h + H - d, H)
        pltpu.make_async_remote_copy(
            src_ref=rf.at[c, src], dst_ref=rf.at[c, src],
            send_sem=rf_send.at[c, d - 1], recv_sem=rf_recv.at[c, d - 1],
            device_id={"hist": src}, device_id_type=MESH,
        ).wait_recv()

    for cc in range(C):
        cols = pl.ds(cc * Nc, Nc)
        for c in range(C):
            rf[cc, h, pl.ds(c * Rc, Rc), :] = pred[c, :, cols] + step_size * acc1[c, :, cols]
        for d in range(1, H):
            rf_copy(cc, d).start()

    base[...] = jnp.zeros_like(base)

    def second(cc):
        cols = pl.ds(cc * Nc, Nc)
        for d in range(1, H):
            rf_wait(cc, d)

        @pl.loop(0, H)
        def _(j):
            split(rf.at[cc, j], xh.at[j], xl.at[j], R)

        a, b = xh[...].reshape(S, Nc), xl[...].reshape(S, Nc)

        @pl.loop(0, H)
        def _(j):
            rows = pl.ds(pl.multiple_of(j * R, R), R)
            left, low = ih[rows, :], il[rows, :]
            s1[rows, :] = mm(left, a) + mm(low, a) + mm(left, b)

        o1_ref[:, cols] = s1[own_rows, :]
        split(s1, p2h, p2l, S, cubic_power)
        if cc == 0:
            for d in range(1, H):
                nf_wait(d)
        a, b = p2h[...], p2l[...]

        @pl.loop(0, H)
        def _(j):
            rows = pl.ds(pl.multiple_of(j * R, R), R)
            left, low = kh[rows, :], kl[rows, :]
            value = mm(left, a) + mm(low, a) + mm(left, b)
            s1[rows, :] = value + nf[j, :, cols] + e2[rows, cols]

        split(s1, p2h, p2l, S)
        split(s1, qh, ql, S, lambda v: step_size * cubic_power(v))
        g2[cc, t] = product(inv2[...], qh[...], ql[...])
        z_own(g2, 1, cc)
        base[:, cols] += product(inv2[...], p2h[...], p2l[...])
        use_two(cc, t)
        z_partner_wait(g2, 1, cc, p)
        use_two(cc, 2 * p + other)

    for cc in range(C):
        second(cc)
        z_step(g2, 1, cc, 1, use_two)
    for s in range(2, Z):
        for cc in range(C):
            z_step(g2, 1, cc, s, use_two)
    o2_ref[...] = base[...]

    for c in range(C):
        for d in range(1, H):
            rs_copy(0, c, d).wait_send()
            rs_copy(1, c, d).wait_send()
            rf_copy(c, d).wait_send()
        z_finish(g1, 0, c)
        z_finish(g2, 1, c)
    for d in range(1, H):
        nf_copy(d).wait_send()


def shards(*operands):
    history, w1 = operands[:2]
    K, N = history.shape
    S = w1.shape[0]
    H, T, C = lax.axis_size("hist"), lax.axis_size("tcol"), 2
    R = S // H
    Rc, Nc, nK, Z = R // C, N // C, K // N, T // 2
    V, D = pltpu.VMEM, pltpu.SemaphoreType.DMA
    return pl.pallas_call(
        functools.partial(kernel, H, T, C),
        out_shape=[jax.ShapeDtypeStruct((R, N), f32)] * 2,
        in_specs=[pl.BlockSpec(memory_space=pl.ANY)] * 9,
        out_specs=[pl.BlockSpec(memory_space=pltpu.VMEM)] * 2,
        scratch_shapes=[
            V((nK, N, N), f32), V((2, C, H, Rc, K), f32),
            V((H, Rc, K), bf16), V((H, Rc, K), bf16),
            V((nK, N, N), bf16), V((nK, N, N), bf16),
            V((T, N, N), bf16), V((T, N, N), bf16),
            V((2, S, S), f32),
            V((S, S), bf16), V((S, S), bf16), V((S, S), bf16), V((S, S), bf16),
            V((R, S), f32), V((R, N), f32), V((S, N), f32),
            V((2, C, H, Rc, N), f32), V((2, C, H - 1, Rc, N), f32),
            V((C, Rc, N), f32), V((C, Rc, N), f32),
            V((C, T, Rc, N), f32), V((C, T, R, Nc), f32),
            V((C, H, R, Nc), f32), V((H, R, N), f32),
            V((H, R, Nc), bf16), V((H, R, Nc), bf16),
            V((S, Nc), f32),
            V((S, Nc), bf16), V((S, Nc), bf16), V((S, Nc), bf16), V((S, Nc), bf16),
            V((R, N), f32),
            D((nK,)), D((2, C, H)), D((T,)), D((5,)),
            D((2, C, H - 1)), D((2, C, H - 1)),
            D((C, H - 1)), D((C, H - 1)), D((H - 1,)), D((H - 1,)),
            D((2, C, Z)), D((2, C, Z)), D((2, C, Z)), D((2, C, Z)), D((2, C, Z)),
        ],
        compiler_params=pltpu.CompilerParams(
            collective_id=0, has_side_effects=True, vmem_limit_bytes=64 * 1024 * 1024 - 65536
        ),
    )(*operands)


def solution(mesh):
    return jax.shard_map(
        shards,
        mesh=mesh,
        in_specs=(
            P("hist", "tcol"),
            P(None, "hist"),
            P(None, "hist"),
            P(),
            P(None, "tcol"),
            P(),
            P(),
            P(None, "tcol"),
            P(None, "tcol"),
        ),
        out_specs=(P("hist", "tcol"), P("hist", "tcol")),
        check_vma=False,
    )
```

time: 247 us -> 90.7 us (0.37)
  waiting for transfers between devices: 153 us -> 0 us
  Pallas kernels: 0 us -> 86.5 us
  matrix products: 72.3 us -> 0 us
  between operations: 14.2 us -> 0.64 us
  other arithmetic: 3.38 us -> 0 us
    reduce_scatter x4 -> x0, waiting for transfers between devices: 92.7 us -> none  [the longest x1 28.8 us: shards(): lax.psum_scatter(matrix_product(memory_weight_first, self_energy_history)...]
    pallas_call x0 -> x1, Pallas kernels: none -> 86.5 us  [shards(): pl.pallas_call(functools.partial(kernel, H, T, C), out_shape=[jax.ShapeDt...]
    dot_general x7 -> x0, matrix products: 72.3 us -> none  [matrix_product(): jnp.dot(left, right, preferred_element_type=jnp.float32, precision=highest)]
    all_gather x2 -> x0, waiting for transfers between devices: 59.7 us -> none  [memory(): lax.all_gather(sigma_rows, 'tcol', axis=1, tiled=True)]
    mul x2 -> x0, other arithmetic: 3.38 us -> none  [cubic_power(): return strength * value * value * value]
  transfers between devices with their start and end apart: 6 -> 0, of which waited for: 6 -> 0; matrix products, arithmetic and copies ran while one was open for 8% -> 0% of each run, Pallas kernels for 0% -> 0%
where the time goes in v1:
time: 90.7 us; the launch traced here: 90.5 us
  Pallas kernels  86.5 us (95%)
  local copies, waits for them, and re-layouts  3.34 us (4%)
    pallas_call x1, Pallas kernels, shards(): pl.pallas_call(functools.partial(kernel, H, T, C), out_shape=[jax.ShapeDt...  86.5 us
    unnamed x2, local copies, waits for them, and re-layouts  3.34 us

profile of v1, /device:TPU:1, one launch (start us, length us, event | category | flops | bytes accessed | tf_op | source)
XLA Modules:
  0.0 90.5 jit_solution(9293010370206452523)
XLA Ops:
  0.6 86.5 %shard_map.104 = (f32[128,512]{1,0:T(8,128)}, f32[128,512]{1,0:T(8,128)}) custom-call(f32[2048,512]{1,0:T(8,128)} %hist_ref.1, f32[512,2048]{1,0:T(8,128)} %w1_ref.1, f32[512,2048]{1,0:T(8,128)} %w2_ref.1, f32[512,512]{1,0:T(8,128)} %link_ref.1, f32[4096,512]{1,0:T(8,128)} %prop_ref.1, f32[512,512]{1,0:T(8,128)} %inv1_ref.1, f32[512,512]{1,0:T(8,128)} %inv2_ref.1, ...), custom_call_target="tpu_custom_call" | custom-call | tf_op jit(solution)/shard_map/pallas_call | solution.py:427
  87.1 1.7 %copy.13 = f32[128,512]{1,0:T(8,128)} copy(f32[128,512]{1,0:T(8,128)} %get-tuple-element.4) | data formatting | bytes 524288
  88.8 1.7 %copy.14 = f32[128,512]{1,0:T(8,128)} copy(f32[128,512]{1,0:T(8,128)} %get-tuple-element.5) | data formatting | bytes 524288

commit v2 on v1

--- a/solution.py
+++ b/solution.py
@@ -38,16 +38,17 @@
     H, T, C,
     hist_ref, w1_ref, w2_ref, link_ref, prop_ref, inv1_ref, inv2_ref, e1_ref, e2_ref,
     o1_ref, o2_ref,
-    hbuf, wbuf, wh, wl, sh, sl, ph, plo, mat, ih, il, kh, kl, inv2, e1, e2,
-    part, rs, pred, acc1, g1, g2, rf, nf, xh, xl, s1, p2h, p2l, qh, ql, base,
-    hsem, wsem, psem, msem, rs_send, rs_recv, rf_send, rf_recv, nf_send, nf_recv,
+    hbuf, wbuf, wh, wl, sh, sl, ph, plo, mat, ih, il, kh, kl, vh, vl, e1, e2,
+    part, rs, pred, acc1, acc2, g1, g2, nsend, nrecv, near, rsend, rf, s1, s2, orecv,
+    ysend, yrecv, bsend, brecv, xh, xl, p2h, p2l, qh, ql,
+    hsem, wsem, psem, msem, rs_send, rs_recv, x_sent, x_got,
     sp, sr, sleft, rz, rp,
 ):
     K, N = hist_ref.shape
     S = w1_ref.shape[0]
     R = S // H
     Rc = R // C
-    Nc = N // C
+    Nh = N // H
     nK = K // N
     Z = T // 2
     h = lax.axis_index("hist")
@@ -84,8 +85,8 @@
         pltpu.make_async_copy(e1_ref.at[own_rows, :], e1, msem.at[0]),
         pltpu.make_async_copy(inv1_ref, mat.at[0], msem.at[1]),
         pltpu.make_async_copy(link_ref, mat.at[1], msem.at[2]),
-        pltpu.make_async_copy(inv2_ref.at[own_rows, :], inv2, msem.at[3]),
-        pltpu.make_async_copy(e2_ref, e2, msem.at[4]),
+        pltpu.make_async_copy(inv2_ref, mat.at[2], msem.at[3]),
+        pltpu.make_async_copy(e2_ref.at[own_rows, :], e2, msem.at[4]),
     )
 
     for kb in range(nK):
@@ -135,20 +136,56 @@
             else:
                 part[w, c] += value
 
-    def rs_copy(w, c, d):
+    def rs_copy(c, d):
         dst = lax.rem(h + d, H)
         return pltpu.make_async_remote_copy(
-            src_ref=part.at[w, c, dst], dst_ref=rs.at[w, c, d - 1],
-            send_sem=rs_send.at[w, c, d - 1], recv_sem=rs_recv.at[w, c, d - 1],
+            src_ref=part.at[0, c, dst], dst_ref=rs.at[c, d - 1],
+            send_sem=rs_send.at[c, d - 1], recv_sem=rs_recv.at[c, d - 1],
             device_id={"hist": dst}, device_id_type=MESH,
         )
 
-    def gathered(w, c):
-        total = part[w, c, h]
+    def gathered(c):
+        total = part[0, c, h]
         for d in range(1, H):
-            rs_copy(w, c, d).wait_recv()
-            total += rs[w, c, d - 1]
+            rs_copy(c, d).wait_recv()
+            total += rs[c, d - 1]
         return total
+
+    def exchange(kind, d, source, target):
+        dst = lax.rem(h + d, H)
+        return pltpu.make_async_remote_copy(
+            src_ref=source(dst), dst_ref=target(h, d),
+            send_sem=x_sent.at[kind, d - 1], recv_sem=x_got.at[kind, d - 1],
+            device_id={"hist": dst}, device_id_type=MESH,
+        )
+
+    def arrived(kind, d, target):
+        src = lax.rem(h + H - d, H)
+        ref = target(src, d)
+        pltpu.make_async_remote_copy(
+            src_ref=ref, dst_ref=ref,
+            send_sem=x_sent.at[kind, d - 1], recv_sem=x_got.at[kind, d - 1],
+            device_id={"hist": src}, device_id_type=MESH,
+        ).wait_recv()
+
+    plans = {}
+    for c in range(C):
+        plans[c] = (
+            lambda dst, c=c: nsend.at[c, dst], lambda src, d, c=c: nrecv.at[c, d - 1])
+        plans[C + c] = (
+            lambda dst, c=c: rsend.at[c, dst], lambda src, d, c=c: rf.at[c, src])
+        plans[2 * C + c] = (
+            lambda dst, c=c: ysend.at[c, dst], lambda src, d, c=c: yrecv.at[c, src])
+    plans[3 * C] = (lambda dst: s1.at[dst], lambda src, d: orecv.at[src])
+    plans[3 * C + 1] = (lambda dst: bsend.at[dst], lambda src, d: brecv.at[src])
+
+    def x_start(kind):
+        for d in range(1, H):
+            exchange(kind, d, *plans[kind]).start()
+
+    def x_wait(kind):
+        for d in range(1, H):
+            arrived(kind, d, plans[kind][1])
 
     def z_copy(g, st, c, q, where):
         block = g.at[c, 2 * q + core]
@@ -255,31 +292,33 @@
         acc1[c] += product(g1[c, b], ph[b], plo[b])
 
     def use_two(c, b):
-        rows = pl.ds(c * Nc, Nc)
-        base[...] += product(g2[c, b], ph[b, rows, :], plo[b, rows, :])
+        acc2[c] += product(g2[c, b], ph[b], plo[b])
 
     history_sum(0, 0)
     pl.semaphore_wait(barrier, H + 2)
 
     for d in range(1, H):
-        rs_copy(0, 0, d).start()
+        rs_copy(0, d).start()
     for c in range(1, C):
         history_sum(0, c)
         for d in range(1, H):
-            rs_copy(0, c, d).start()
+            rs_copy(c, d).start()
 
     small[0].wait()
 
     def begin_one(c):
-        value = gathered(0, c) + e1[pl.ds(c * Rc, Rc), :]
+        value = gathered(c) + e1[pl.ds(c * Rc, Rc), :]
         pred[c] = value
         g1[c, t] = cubic_power(value)
         z_own(g1, 0, c)
 
+    small[4].wait()
     for c in range(C):
         history_sum(1, c)
-        for d in range(1, H):
-            rs_copy(1, c, d).start()
+        part[1, c, h] += e2[pl.ds(c * Rc, Rc), :]
+        for j in range(H):
+            nsend[c, j] = part[1, c, :, :, j * Nh:(j + 1) * Nh]
+        x_start(c)
         if c == 0:
             begin_one(0)
 
@@ -302,118 +341,127 @@
         local_one(c)
         z_step(g1, 0, c, 1, use_one)
 
-    for copy in small[1:]:
+    for copy in small[1:4]:
         copy.wait()
     split(mat.at[0], ih, il, S)
     split(mat.at[1], kh, kl, S)
-
-    def nf_copy(d):
-        dst = lax.rem(h + d, H)
-        return pltpu.make_async_remote_copy(
-            src_ref=nf.at[h], dst_ref=nf.at[h],
-            send_sem=nf_send.at[d - 1], recv_sem=nf_recv.at[d - 1],
-            device_id={"hist": dst}, device_id_type=MESH,
-        )
-
-    def nf_wait(d):
-        src = lax.rem(h + H - d, H)
-        pltpu.make_async_remote_copy(
-            src_ref=nf.at[src], dst_ref=nf.at[src],
-            send_sem=nf_send.at[d - 1], recv_sem=nf_recv.at[d - 1],
-            device_id={"hist": src}, device_id_type=MESH,
-        ).wait_recv()
+    split(mat.at[2], vh, vl, S)
+
+    def send_right(c):
+        value = pred[c] + step_size * acc1[c]
+        for j in range(H):
+            rsend[c, j] = value[:, j * Nh:(j + 1) * Nh]
+        x_start(C + c)
+        rf[c, h] = rsend[c, h]
+
+    def sum_near():
+        for c in range(C):
+            x_wait(c)
+            total = nsend[c, h]
+            for d in range(1, H):
+                total += nrecv[c, d - 1]
+            near[:, c] = total
 
     for s in range(2, Z):
         for c in range(C):
             z_step(g1, 0, c, s, use_one)
-        if s == max(2, Z // 2):
-            for c in range(C):
-                nf[h, pl.ds(c * Rc, Rc), :] = gathered(1, c)
-            for d in range(1, H):
-                nf_copy(d).start()
-
-    def rf_copy(c, d):
-        dst = lax.rem(h + d, H)
-        return pltpu.make_async_remote_copy(
-            src_ref=rf.at[c, h], dst_ref=rf.at[c, h],
-            send_sem=rf_send.at[c, d - 1], recv_sem=rf_recv.at[c, d - 1],
-            device_id={"hist": dst}, device_id_type=MESH,
-        )
-
-    def rf_wait(c, d):
-        src = lax.rem(h + H - d, H)
-        pltpu.make_async_remote_copy(
-            src_ref=rf.at[c, src], dst_ref=rf.at[c, src],
-            send_sem=rf_send.at[c, d - 1], recv_sem=rf_recv.at[c, d - 1],
-            device_id={"hist": src}, device_id_type=MESH,
-        ).wait_recv()
-
-    for cc in range(C):
-        cols = pl.ds(cc * Nc, Nc)
+            if s == Z - 1:
+                send_right(c)
+    if Z == 2:
         for c in range(C):
-            rf[cc, h, pl.ds(c * Rc, Rc), :] = pred[c, :, cols] + step_size * acc1[c, :, cols]
-        for d in range(1, H):
-            rf_copy(cc, d).start()
-
-    base[...] = jnp.zeros_like(base)
-
-    def second(cc):
-        cols = pl.ds(cc * Nc, Nc)
-        for d in range(1, H):
-            rf_wait(cc, d)
+            send_right(c)
+    sum_near()
+
+    for c in range(C):
+        x_wait(C + c)
 
         @pl.loop(0, H)
         def _(j):
-            split(rf.at[cc, j], xh.at[j], xl.at[j], R)
-
-        a, b = xh[...].reshape(S, Nc), xl[...].reshape(S, Nc)
-
-        @pl.loop(0, H)
-        def _(j):
-            rows = pl.ds(pl.multiple_of(j * R, R), R)
-            left, low = ih[rows, :], il[rows, :]
-            s1[rows, :] = mm(left, a) + mm(low, a) + mm(left, b)
-
-        o1_ref[:, cols] = s1[own_rows, :]
-        split(s1, p2h, p2l, S, cubic_power)
-        if cc == 0:
-            for d in range(1, H):
-                nf_wait(d)
-        a, b = p2h[...], p2l[...]
-
-        @pl.loop(0, H)
-        def _(j):
-            rows = pl.ds(pl.multiple_of(j * R, R), R)
-            left, low = kh[rows, :], kl[rows, :]
-            value = mm(left, a) + mm(low, a) + mm(left, b)
-            s1[rows, :] = value + nf[j, :, cols] + e2[rows, cols]
-
-        split(s1, p2h, p2l, S)
-        split(s1, qh, ql, S, lambda v: step_size * cubic_power(v))
-        g2[cc, t] = product(inv2[...], qh[...], ql[...])
-        z_own(g2, 1, cc)
-        base[:, cols] += product(inv2[...], p2h[...], p2l[...])
-        use_two(cc, t)
-        z_partner_wait(g2, 1, cc, p)
-        use_two(cc, 2 * p + other)
-
-    for cc in range(C):
-        second(cc)
-        z_step(g2, 1, cc, 1, use_two)
+            a, b = halves(rf[c, j])
+            xh[j, c] = a
+            xl[j, c] = b
+
+    def apply(high, low, j, a, b):
+        rows = pl.ds(pl.multiple_of(j * R, R), R)
+        left, rest = high[rows, :], low[rows, :]
+        return mm(left, a) + mm(rest, a) + mm(left, b)
+
+    a, b = xh[...].reshape(S, Nh), xl[...].reshape(S, Nh)
+
+    @pl.loop(0, H)
+    def _(j):
+        value = apply(ih, il, j, a, b)
+        s1[j] = value
+        p2h[j], p2l[j] = halves(cubic_power(value))
+
+    a, b = p2h[...].reshape(S, Nh), p2l[...].reshape(S, Nh)
+
+    @pl.loop(0, H)
+    def _(j):
+        value = apply(kh, kl, j, a, b) + near[j].reshape(R, Nh)
+        s2[j] = value
+        qh[j], ql[j] = halves(step_size * cubic_power(value))
+
+    a, b = qh[...].reshape(S, Nh), ql[...].reshape(S, Nh)
+
+    @pl.loop(0, H)
+    def _(j):
+        value = apply(vh, vl, j, a, b)
+        for c in range(C):
+            ysend[c, j] = value[c * Rc:(c + 1) * Rc, :]
+
+    for c in range(C):
+        x_start(2 * C + c)
+        yrecv[c, h] = ysend[c, h]
+    x_start(3 * C)
+    orecv[h] = s1[h]
+
+    @pl.loop(0, H)
+    def _(j):
+        p2h[j], p2l[j] = halves(s2[j])
+
+    a, b = p2h[...].reshape(S, Nh), p2l[...].reshape(S, Nh)
+
+    @pl.loop(0, H)
+    def _(j):
+        bsend[j] = apply(vh, vl, j, a, b)
+
+    def begin_two(c):
+        x_wait(2 * C + c)
+        g2[c, t] = jnp.concatenate([yrecv[c, j] for j in range(H)], axis=1)
+        z_own(g2, 1, c)
+
+    def local_two(c):
+        acc2[c] = product(g2[c, t], ph[t], plo[t])
+        z_partner_wait(g2, 1, c, p)
+        use_two(c, 2 * p + other)
+
+    for c in range(C):
+        begin_two(c)
+    x_start(3 * C + 1)
+    brecv[h] = bsend[h]
+    for c in range(C):
+        local_two(c)
+        z_step(g2, 1, c, 1, use_two)
+    x_wait(3 * C)
+    for j in range(H):
+        o1_ref[:, j * Nh:(j + 1) * Nh] = orecv[j]
     for s in range(2, Z):
-        for cc in range(C):
-            z_step(g2, 1, cc, s, use_two)
-    o2_ref[...] = base[...]
+        for c in range(C):
+            z_step(g2, 1, c, s, use_two)
+    x_wait(3 * C + 1)
+    for c in range(C):
+        rows = pl.ds(c * Rc, Rc)
+        o2_ref[rows, :] = acc2[c] + jnp.concatenate([brecv[j, rows, :] for j in range(H)], axis=1)
 
     for c in range(C):
         for d in range(1, H):
-            rs_copy(0, c, d).wait_send()
-            rs_copy(1, c, d).wait_send()
-            rf_copy(c, d).wait_send()
+            rs_copy(c, d).wait_send()
         z_finish(g1, 0, c)
         z_finish(g2, 1, c)
-    for d in range(1, H):
-        nf_copy(d).wait_send()
+    for kind in range(3 * C + 2):
+        for d in range(1, H):
+            exchange(kind, d, *plans[kind]).wait_send()
 
 
 def shards(*operands):
@@ -422,7 +470,7 @@
     S = w1.shape[0]
     H, T, C = lax.axis_size("hist"), lax.axis_size("tcol"), 2
     R = S // H
-    Rc, Nc, nK, Z = R // C, N // C, K // N, T // 2
+    Rc, Nh, nK, Z = R // C, N // H, K // N, T // 2
     V, D = pltpu.VMEM, pltpu.SemaphoreType.DMA
     return pl.pallas_call(
         functools.partial(kernel, H, T, C),
@@ -434,20 +482,21 @@
             V((H, Rc, K), bf16), V((H, Rc, K), bf16),
             V((nK, N, N), bf16), V((nK, N, N), bf16),
             V((T, N, N), bf16), V((T, N, N), bf16),
-            V((2, S, S), f32),
-            V((S, S), bf16), V((S, S), bf16), V((S, S), bf16), V((S, S), bf16),
-            V((R, S), f32), V((R, N), f32), V((S, N), f32),
-            V((2, C, H, Rc, N), f32), V((2, C, H - 1, Rc, N), f32),
-            V((C, Rc, N), f32), V((C, Rc, N), f32),
-            V((C, T, Rc, N), f32), V((C, T, R, Nc), f32),
-            V((C, H, R, Nc), f32), V((H, R, N), f32),
-            V((H, R, Nc), bf16), V((H, R, Nc), bf16),
-            V((S, Nc), f32),
-            V((S, Nc), bf16), V((S, Nc), bf16), V((S, Nc), bf16), V((S, Nc), bf16),
-            V((R, N), f32),
+            V((3, S, S), f32),
+            *[V((S, S), bf16)] * 6,
+            V((R, N), f32), V((R, N), f32),
+            V((2, C, H, Rc, N), f32), V((C, H - 1, Rc, N), f32),
+            V((C, Rc, N), f32), V((C, Rc, N), f32), V((C, Rc, N), f32),
+            V((C, T, Rc, N), f32), V((C, T, Rc, N), f32),
+            V((C, H, H, Rc, Nh), f32), V((C, H - 1, H, Rc, Nh), f32), V((H, C, Rc, Nh), f32),
+            V((C, H, Rc, Nh), f32), V((C, H, Rc, Nh), f32),
+            V((H, R, Nh), f32), V((H, R, Nh), f32), V((H, R, Nh), f32),
+            V((C, H, Rc, Nh), f32), V((C, H, Rc, Nh), f32),
+            V((H, R, Nh), f32), V((H, R, Nh), f32),
+            V((H, C, Rc, Nh), bf16), V((H, C, Rc, Nh), bf16),
+            *[V((H, R, Nh), bf16)] * 4,
             D((nK,)), D((2, C, H)), D((T,)), D((5,)),
-            D((2, C, H - 1)), D((2, C, H - 1)),
-            D((C, H - 1)), D((C, H - 1)), D((H - 1,)), D((H - 1,)),
+            D((C, H - 1)), D((C, H - 1)), D((3 * C + 2, H - 1)), D((3 * C + 2, H - 1)),
             D((2, C, Z)), D((2, C, Z)), D((2, C, Z)), D((2, C, Z)), D((2, C, Z)),
         ],
         compiler_params=pltpu.CompilerParams(

time: 90.7 us -> 77.6 us (0.86)
  Pallas kernels: 86.5 us -> 73.5 us
    pallas_call x1, Pallas kernels: 86.5 us -> 73.5 us  [shards(): pl.pallas_call(functools.partial(kernel, H, T, C), out_shape=[jax.ShapeDt...]
where the time goes in v2:
time: 77.6 us; the launch traced here: 77.4 us
  Pallas kernels  73.5 us (95%)
  local copies, waits for them, and re-layouts  3.34 us (4%)
    pallas_call x1, Pallas kernels, shards(): pl.pallas_call(functools.partial(kernel, H, T, C), out_shape=[jax.ShapeDt...  73.5 us
    unnamed x2, local copies, waits for them, and re-layouts  3.34 us

profile of v2, /device:TPU:1, one launch (start us, length us, event | category | flops | bytes accessed | tf_op | source)
XLA Modules:
  0.0 77.4 jit_solution(18359121691782394092)
XLA Ops:
  0.6 73.5 %shard_map.104 = (f32[128,512]{1,0:T(8,128)}, f32[128,512]{1,0:T(8,128)}) custom-call(f32[2048,512]{1,0:T(8,128)} %hist_ref.1, f32[512,2048]{1,0:T(8,128)} %w1_ref.1, f32[512,2048]{1,0:T(8,128)} %w2_ref.1, f32[512,512]{1,0:T(8,128)} %link_ref.1, f32[4096,512]{1,0:T(8,128)} %prop_ref.1, f32[512,512]{1,0:T(8,128)} %inv1_ref.1, f32[512,512]{1,0:T(8,128)} %inv2_ref.1, ...), custom_call_target="tpu_custom_call" | custom-call | tf_op jit(solution)/shard_map/pallas_call | solution.py:475
  74.1 1.7 %copy.13 = f32[128,512]{1,0:T(8,128)} copy(f32[128,512]{1,0:T(8,128)} %get-tuple-element.4) | data formatting | bytes 524288
  75.8 1.7 %copy.14 = f32[128,512]{1,0:T(8,128)} copy(f32[128,512]{1,0:T(8,128)} %get-tuple-element.5) | data formatting | bytes 524288

commit v3 on v2

--- a/solution.py
+++ b/solution.py
@@ -312,34 +312,35 @@
         g1[c, t] = cubic_power(value)
         z_own(g1, 0, c)
 
+    for b in range(T):
+        p_copy(b).wait()
+        split(hbuf.at[b % nK], ph.at[b], plo.at[b], N)
+        if b + nK < T:
+            p_copy(b + nK).start()
+
     small[4].wait()
-    for c in range(C):
+
+    def near_sums(c):
         history_sum(1, c)
         part[1, c, h] += e2[pl.ds(c * Rc, Rc), :]
         for j in range(H):
             nsend[c, j] = part[1, c, :, :, j * Nh:(j + 1) * Nh]
         x_start(c)
-        if c == 0:
-            begin_one(0)
-
-    for b in range(T):
-        p_copy(b).wait()
-        split(hbuf.at[b % nK], ph.at[b], plo.at[b], N)
-        if b + nK < T:
-            p_copy(b + nK).start()
 
     def local_one(c):
         acc1[c] = product(g1[c, t], ph[t], plo[t])
         z_partner_wait(g1, 0, c, p)
         use_one(c, 2 * p + other)
 
-    local_one(0)
+    begin_one(0)
+    near_sums(0)
     for c in range(1, C):
-        if c == 1:
-            z_step(g1, 0, 0, 1, use_one)
         begin_one(c)
+    for c in range(C):
         local_one(c)
         z_step(g1, 0, c, 1, use_one)
+    for c in range(1, C):
+        near_sums(c)
 
     for copy in small[1:4]:
         copy.wait()

time: 77.6 us -> 77.6 us (level)
  no operation moved by 1% of the time
where the time goes in v3:
time: 77.6 us; the launch traced here: 77.4 us
  Pallas kernels  73.4 us (95%)
  local copies, waits for them, and re-layouts  3.34 us (4%)
    pallas_call x1, Pallas kernels, shards(): pl.pallas_call(functools.partial(kernel, H, T, C), out_shape=[jax.ShapeDt...  73.4 us
    unnamed x2, local copies, waits for them, and re-layouts  3.34 us

profile of v3, /device:TPU:1, one launch (start us, length us, event | category | flops | bytes accessed | tf_op | source)
XLA Modules:
  0.0 77.4 jit_solution(11594095974145463725)
XLA Ops:
  0.6 73.4 %shard_map.104 = (f32[128,512]{1,0:T(8,128)}, f32[128,512]{1,0:T(8,128)}) custom-call(f32[2048,512]{1,0:T(8,128)} %hist_ref.1, f32[512,2048]{1,0:T(8,128)} %w1_ref.1, f32[512,2048]{1,0:T(8,128)} %w2_ref.1, f32[512,512]{1,0:T(8,128)} %link_ref.1, f32[4096,512]{1,0:T(8,128)} %prop_ref.1, f32[512,512]{1,0:T(8,128)} %inv1_ref.1, f32[512,512]{1,0:T(8,128)} %inv2_ref.1, ...), custom_call_target="tpu_custom_call" | custom-call | tf_op jit(solution)/shard_map/pallas_call | solution.py:476
  74.1 1.7 %copy.13 = f32[128,512]{1,0:T(8,128)} copy(f32[128,512]{1,0:T(8,128)} %get-tuple-element.4) | data formatting | bytes 524288
  75.8 1.7 %copy.14 = f32[128,512]{1,0:T(8,128)} copy(f32[128,512]{1,0:T(8,128)} %get-tuple-element.5) | data formatting | bytes 524288
